TPU v7x, 512 devices: a whole 4x8x8 slice. The times are simulated.
512 devices in a mesh: region: 32 (over x, y), shard: 16 (over z, core).
Axes of the slice: x: 4, y: 8, z: 8, core: 2. Of those that a mesh axis runs over, the one named last changes fastest.
Arguments:
- state_anom: float32 [524288, 256], P(('region', 'shard')), may hold values from -6 to 6
- state_mean: float32 [524288], P(('region', 'shard')), may hold values from -6 to 6
- obs_anom: float32 [64, 512, 256], P('region', 'shard'), may hold values from -6 to 6
- obs_depart: float32 [64, 512], P('region', 'shard'), may hold values from -6 to 6
- obs_var: float32 [64, 512], P('region', 'shard'), may hold values from 0.5 to 2
- taper_levels: float32 [8], replicated, may hold values from 0 to 1
- state_taper: int32 [4096, 256], P(('region', 'shard')), may hold values from 0 to 7
- obs_taper: int32 [256, 256], P('region'), may hold values from 0 to 7
- batch_order: int32 [3], replicated, may hold values from 0 to 63, as said below
Outputs:
- post_anom: float32 [524288, 256], P(('region', 'shard'))
- post_mean: float32 [524288], P(('region', 'shard'))
- post_obs_anom: float32 [64, 512, 256], P('region', 'shard')
- post_obs_depart: float32 [64, 512], P('region', 'shard')
Inputs may be any that keep to these rules, and one draw needn't show every extreme that they name: `batch_order`: 3 distinct batch numbers; batch q lies in region q // 2; the first and the last batch number both occur.
All inputs are finite; a program needn't handle non-finite values.
Results may differ from a plain program's by a relative error of at most 0.0001.
Values sent between devices are 32-bit elements; how exact they have to be, the bound alone decides.
No kernel may reach another device: no remote copies, remote signals or barrier semaphores. Data moves between devices by JAX's collectives and lax.ppermute only.
A program may use at most 64 MiB of HBM per device.

v0:
```python
import jax
import jax.numpy as jnp
from jax import lax
from jax.sharding import PartitionSpec as P

M = 256
P_SIZE = 512
TAPER_BLOCK = 128
NB = 3
KB = 2
highest = lax.Precision.HIGHEST


def from_root(block, axis, source):
    block = jnp.where(lax.axis_index(axis) == source, block, jnp.zeros_like(block))
    return lax.psum(block, axis)


def factorize(anomalies, departs, variances):
    product = jnp.dot(anomalies, anomalies.T, precision=highest, preferred_element_type=jnp.float32)
    system = product / (M - 1) + jnp.diag(variances)
    lower_factor = jnp.linalg.cholesky(system)
    shifted = lower_factor + jnp.diag(jnp.sqrt(variances))
    solved = lax.linalg.triangular_solve(shifted, anomalies, left_side=True, lower=True)
    increments = lax.linalg.triangular_solve(
        lower_factor, solved, left_side=True, lower=True, transpose_a=True
    )
    first = lax.linalg.triangular_solve(lower_factor, departs[:, None], left_side=True, lower=True)
    weights = lax.linalg.triangular_solve(
        lower_factor, first, left_side=True, lower=True, transpose_a=True
    )
    return (increments, weights[:, 0])


def lookup(levels, index):
    levels_count = levels.shape[0]
    onehot = (index[..., None] == jnp.arange(levels_count, dtype=jnp.int32)).astype(jnp.float32)
    return jnp.sum(onehot * levels, axis=-1)


def covariance(rows, batch_rows):
    product = lax.dot_general(
        rows,
        batch_rows,
        (((1,), (1,)), ((), ())),
        precision=highest,
        preferred_element_type=jnp.float32,
    )
    return product / (M - 1)


def apply_rows(covar, increments, weights):
    delta_rows = jnp.dot(covar, increments, precision=highest, preferred_element_type=jnp.float32)
    delta_mean = jnp.dot(covar, weights, precision=highest, preferred_element_type=jnp.float32)
    return (delta_rows, delta_mean)


def per_device(
    state_anom,
    state_mean,
    obs_anom,
    obs_depart,
    obs_var,
    taper_levels,
    state_taper,
    obs_taper,
    batch_order,
):
    shard_pos = lax.axis_index("shard")
    pieces = obs_anom.shape[1]
    blocks = P_SIZE // TAPER_BLOCK
    obs_rows = obs_anom.shape[0] * pieces
    state_rows = state_anom.shape[0]
    row_block = (
        jnp.arange(KB, dtype=jnp.int32)[:, None] * P_SIZE
        + shard_pos * pieces
        + jnp.arange(pieces, dtype=jnp.int32)[None, :]
    ).reshape(obs_rows) // TAPER_BLOCK
    anomaly = state_anom
    mean_state = state_mean
    obs_now = obs_anom.reshape(obs_rows, M)
    depart_now = obs_depart.reshape(obs_rows)
    for section_idx in range(NB):
        batch_id = batch_order[section_idx]
        owner_id = batch_id // KB
        local_id = batch_id % KB
        rows_piece = lax.dynamic_slice_in_dim(obs_now, local_id * pieces, pieces, 0)
        depart_piece = lax.dynamic_slice_in_dim(depart_now, local_id * pieces, pieces, 0)
        var_piece = lax.dynamic_index_in_dim(obs_var, local_id, 0, keepdims=False)
        sent_rows, sent_depart, sent_var = (
            from_root(rows_piece, "region", owner_id),
            from_root(depart_piece, "region", owner_id),
            from_root(var_piece, "region", owner_id),
        )
        batch_rows, departs, variances = (
            lax.all_gather(sent_rows, "shard", axis=0, tiled=True),
            lax.all_gather(sent_depart, "shard", axis=0, tiled=True),
            lax.all_gather(sent_var, "shard", axis=0, tiled=True),
        )
        increments, weights = factorize(batch_rows, departs, variances)
        state_cols = lax.dynamic_slice_in_dim(state_taper, batch_id * blocks, blocks, 1)
        state_weights = lookup(taper_levels, state_cols)
        covar = covariance(anomaly, batch_rows)
        covar = (
            covar.reshape(state_rows // TAPER_BLOCK, TAPER_BLOCK, blocks, TAPER_BLOCK)
            * state_weights[:, None, :, None]
        )
        covar = covar.reshape(state_rows, P_SIZE)
        delta_rows, delta_mean = apply_rows(covar, increments, weights)
        obs_cols = lax.dynamic_slice_in_dim(obs_taper, batch_id * blocks, blocks, 1)
        obs_weights = lookup(taper_levels, jnp.take(obs_cols, row_block, axis=0))
        covar_obs = (
            covariance(obs_now, batch_rows).reshape(obs_rows, blocks, TAPER_BLOCK)
            * obs_weights[:, :, None]
        )
        covar_obs = covar_obs.reshape(obs_rows, P_SIZE)
        delta_obs, delta_depart = apply_rows(covar_obs, increments, weights)
        anomaly = anomaly - delta_rows
        mean_state = mean_state + delta_mean
        obs_now = obs_now - delta_obs
        depart_now = depart_now - delta_depart
    return (
        anomaly,
        mean_state,
        obs_now.reshape(obs_anom.shape),
        depart_now.reshape(obs_depart.shape),
    )


def solution(mesh):
    placed = (
        P(("region", "shard"), None),
        P(("region", "shard")),
        P("region", "shard", None),
        P("region", "shard"),
        P("region", "shard"),
        P(),
        P(("region", "shard"), None),
        P("region", None),
        P(),
    )
    return jax.shard_map(
        per_device,
        mesh=mesh,
        in_specs=placed,
        out_specs=(
            P(("region", "shard"), None),
            P(("region", "shard")),
            P("region", "shard", None),
            P("region", "shard"),
        ),
        check_vma=False,
    )
```

profile of v0, /device:TPU:1, one launch (start us, length us, event | category | flops | bytes accessed | tf_op | source)
XLA Modules:
  0.0 1229.0 jit_solution(11346918617934155445)
XLA Ops:
  12.8 116.3 %all-reduce.9 = (f32[32,256]{1,0:T(8,128)S(1)}, f32[32]{0:T(128)S(1)}, f32[32]{0:T(128)S(1)}) all-reduce(f32[32,256]{1,0:T(8,128)S(1)} %dynamic-slice_select_fusion.2, f32[32]{0:T(128)S(1)} %get-tuple-element.312, f32[32]{0:T(128)S(1)} %broadcast_select_fusion.5), channel_id=1, replica_groups=mesh['region'=32,'shard'=16] {'region'}, use_global_device_ids=true, to_apply=%region_0.1 | all-reduce | flops 8256 | bytes 66048 | tf_op jit(solution)/shard_map/psum | solution.py:16
  131.5 57.6 %all-reduce.12 = (f32[512]{0:T(512)S(1)}, f32[512]{0:T(512)S(1)}) all-reduce(f32[512]{0:T(512)S(1)} %dynamic-update-slice.30, f32[512]{0:T(512)S(1)} %dynamic-update-slice.33), channel_id=1, replica_groups=mesh['region'=32,'shard'=16] {'shard'}, use_global_device_ids=true, to_apply=%add.1 | all-reduce | flops 1024 | bytes 8192
  189.1 15.9 %all_gather.27 = f32[512,256]{1,0:T(8,128)S(1)} all-gather(f32[32,256]{1,0:T(8,128)S(1)} %get-tuple-element.258), channel_id=1, replica_groups=mesh['region'=32,'shard'=16] {'shard'}, dimensions={0}, use_global_device_ids=true | all-gather | bytes 557056 | tf_op jit(solution)/shard_map/all_gather | solution.py:96
  207.6 11.7 cholesky.374
  219.3 9.8 custom-call.46
  231.7 11.7 cholesky.393
  246.0 9.8 custom-call.47
  257.7 11.7 cholesky.414
  270.9 9.8 custom-call.48
  282.4 12.1 cholesky.431
  297.2 8.4 while.25
  305.7 39.3 %custom-call.50 = f32[4,128,128]{1,2,0:T(8,128)S(1)} custom-call(f32[4,128,128]{2,1,0:T(8,128)S(1)} %get-tuple-element.91), custom_call_target="InvertDiagBlocksLowerTriangular" | custom-call | tf_op jit(solution)/shard_map/triangular_solve/custom-call.8 | solution.py:25
  354.8 11.6 while.24
  355.4 2.2 dynamic-slice.53
  358.4 2.2 dynamic-slice.53
  361.3 2.2 dynamic-slice.53
  364.2 2.1 dynamic-slice.53
  366.5 39.3 %custom-call.49 = f32[4,128,128]{1,2,0:T(8,128)S(1)} custom-call(f32[4,128,128]{2,1,0:T(8,128)S(1)} %get-tuple-element.90), custom_call_target="InvertDiagBlocksLowerTriangular" | custom-call | tf_op jit(solution)/shard_map/triangular_solve/custom-call.3 | solution.py:24
  413.5 110.3 %all-reduce.8 = (f32[32,256]{1,0:T(8,128)S(1)}, f32[32]{0:T(128)S(1)}, f32[32]{0:T(128)S(1)}) all-reduce(f32[32,256]{1,0:T(8,128)S(1)} %dynamic-slice_select_fusion.1, f32[32]{0:T(128)S(1)} %copy-done.62, f32[32]{0:T(128)S(1)} %broadcast_select_fusion.4), channel_id=1, replica_groups=mesh['region'=32,'shard'=16] {'region'}, use_global_device_ids=true, to_apply=%region_12.17 | all-reduce | flops 8256 | bytes 66048 | tf_op jit(solution)/shard_map/psum | solution.py:16
  524.2 51.0 %all-reduce.11 = (f32[512]{0:T(512)S(1)}, f32[512]{0:T(512)}) all-reduce(f32[512]{0:T(512)S(1)} %dynamic-update-slice.31, f32[512]{0:T(512)S(1)} %dynamic-update-slice.34), channel_id=1, replica_groups=mesh['region'=32,'shard'=16] {'shard'}, use_global_device_ids=true, to_apply=%add.2 | all-reduce | flops 1024 | bytes 8192
  575.2 16.4 %all_gather.29 = f32[512,256]{1,0:T(8,128)S(1)} all-gather(f32[32,256]{1,0:T(8,128)S(1)} %get-tuple-element.255), channel_id=1, replica_groups=mesh['region'=32,'shard'=16] {'shard'}, dimensions={0}, use_global_device_ids=true | all-gather | bytes 557056 | tf_op jit(solution)/shard_map/all_gather | solution.py:96
  594.2 11.7 cholesky.446
  605.9 9.8 custom-call.51
  618.3 11.7 cholesky.465
  633.6 9.8 custom-call.52
  645.2 11.7 cholesky.486
  658.4 9.8 custom-call.53
  669.8 11.9 cholesky.503
  684.5 8.4 while.27
  692.9 39.3 %custom-call.55 = f32[4,128,128]{1,2,0:T(8,128)S(1)} custom-call(f32[4,128,128]{2,1,0:T(8,128)S(1)} %get-tuple-element.93), custom_call_target="InvertDiagBlocksLowerTriangular" | custom-call | tf_op jit(solution)/shard_map/triangular_solve/custom-call.8 | solution.py:25
  737.0 12.5 %while.26 = (s32[]{:T(128)}, f32[512,512]{0,1:T(8,128)}, s32[4,2]{0,1:T(2,128)S(1)}, f32[4,128,128]{2,1,0:T(8,128)S(1)}, s32[]{:T(128)}) while((s32[]{:T(128)}, f32[512,512]{0,1:T(8,128)}, s32[4,2]{0,1:T(2,128)S(1)}, f32[4,128,128]{2,1,0:T(8,128)S(1)}, s32[]{:T(128)}) %tuple.196), condition=%wide.while_cond.clone, body=%wide.while_body.clone.sunk | while | flops 2 | bytes 393321 | solution.py:24
  737.7 2.3 dynamic-slice.57
  740.8 2.3 dynamic-slice.57
  743.9 2.3 dynamic-slice.57
  747.1 2.3 dynamic-slice.57
  750.2 40.1 %custom-call.54 = f32[4,128,128]{1,2,0:T(8,128)S(1)} custom-call(f32[4,128,128]{2,1,0:T(8,128)} %copy-done.24), custom_call_target="InvertDiagBlocksLowerTriangular" | custom-call | tf_op jit(solution)/shard_map/triangular_solve/custom-call.3 | solution.py:24
  801.3 110.3 %all-reduce.7 = (f32[32,256]{1,0:T(8,128)S(1)}, f32[32]{0:T(128)S(1)}, f32[32]{0:T(128)S(1)}) all-reduce(f32[32,256]{1,0:T(8,128)S(1)} %dynamic-slice_select_fusion, f32[32]{0:T(128)S(1)} %copy-done.61, f32[32]{0:T(128)S(1)} %copy-done.63), channel_id=1, replica_groups=mesh['region'=32,'shard'=16] {'region'}, use_global_device_ids=true, to_apply=%region_16.21 | all-reduce | flops 8256 | bytes 66048 | tf_op jit(solution)/shard_map/psum | solution.py:16
  911.6 44.7 %all_gather.31 = f32[512,256]{1,0:T(8,128)S(1)} all-gather(f32[32,256]{1,0:T(8,128)S(1)} %get-tuple-element.252), channel_id=1, replica_groups=mesh['region'=32,'shard'=16] {'shard'}, dimensions={0}, use_global_device_ids=true | all-gather | bytes 557056 | tf_op jit(solution)/shard_map/all_gather | solution.py:96
  958.3 24.0 %all-reduce.10 = (f32[512]{0:T(512)S(1)}, f32[512]{0:T(512)}) all-reduce(f32[512]{0:T(512)S(1)} %dynamic-update-slice.32, f32[512]{0:T(512)S(1)} %dynamic-update-slice.35), channel_id=1, replica_groups=mesh['region'=32,'shard'=16] {'shard'}, use_global_device_ids=true, to_apply=%add.3 | all-reduce | flops 1024 | bytes 8192
  987.1 11.7 cholesky.518
  998.8 9.8 custom-call.56
  1011.2 11.7 cholesky.537
  1028.2 10.6 custom-call.57
  1040.7 11.7 cholesky.558
  1053.8 9.8 custom-call.58
  1065.3 11.9 cholesky.575
  1080.3 12.5 %while.29 = (s32[]{:T(128)}, f32[512,512]{0,1:T(8,128)}, s32[4,2]{0,1:T(2,128)S(1)}, f32[4,128,128]{2,1,0:T(8,128)S(1)}, s32[]{:T(128)}) while((s32[]{:T(128)}, f32[512,512]{0,1:T(8,128)}, s32[4,2]{0,1:T(2,128)S(1)}, f32[4,128,128]{2,1,0:T(8,128)S(1)}, s32[]{:T(128)}) %tuple.197), condition=%wide.while_cond.1.clone.1, body=%wide.while_body.1.clone.1.sunk | while | flops 2 | bytes 393321 | solution.py:25
  1081.0 2.3 dynamic-slice.63
  1084.1 2.3 dynamic-slice.63
  1087.2 2.3 dynamic-slice.63
  1090.4 2.3 dynamic-slice.63
  1092.8 39.3 %custom-call.60 = f32[4,128,128]{1,2,0:T(8,128)S(1)} custom-call(f32[4,128,128]{2,1,0:T(8,128)S(1)} %get-tuple-element.95), custom_call_target="InvertDiagBlocksLowerTriangular" | custom-call | tf_op jit(solution)/shard_map/triangular_solve/custom-call.8 | solution.py:25
  1141.3 11.9 while.28
  1142.0 2.3 dynamic-slice.61
  1145.0 2.3 dynamic-slice.61
  1147.9 2.3 dynamic-slice.61
  1150.9 2.2 dynamic-slice.61
  1153.3 39.7 %custom-call.59 = f32[4,128,128]{1,2,0:T(8,128)S(1)} custom-call(f32[4,128,128]{2,1,0:T(8,128)S(1)} %get-tuple-element.94), custom_call_target="InvertDiagBlocksLowerTriangular" | custom-call | tf_op jit(solution)/shard_map/triangular_solve/custom-call.3 | solution.py:24
  1207.4 2.3 bitcast_multiply_fusion.2
  1211.0 3.6 convolution_subtract_fusion.2
  1215.0 2.2 bitcast_multiply_fusion.1
  1217.3 1.9 fusion.267
  1221.4 2.0 bitcast_multiply_fusion
  1226.0 2.8 convolution_subtract_fusion
  (486 shorter events, 142.1 us)
Async XLA Ops:
  206.6 1.0 copy-start.2
  297.2 52.8 %copy-start.31 = (s32[8,256]{1,0:T(8,128)S(1)}, s32[8,256]{1,0:T(8,128)}, u32[]{:S(2)}) copy-start(s32[8,256]{1,0:T(8,128)} %param.27) | copy-start | bytes 24580
  297.2 52.8 %copy-start.32 = (s32[8,256]{1,0:T(8,128)S(1)}, s32[8,256]{1,0:T(8,128)}, u32[]{:S(2)}) copy-start(s32[8,256]{1,0:T(8,128)} %param.26) | copy-start | bytes 24580
  297.2 55.7 %copy-start.64 = (f32[8]{0:T(128)S(1)}, f32[8]{0:T(128)}, u32[]{:S(2)}) copy-start(f32[8]{0:T(128)} %param.25) | copy-start | bytes 100
  297.2 56.6 %copy-start.25 = (f32[2,32,256]{2,1,0:T(8,128)S(1)}, f32[2,32,256]{2,1,0:T(8,128)}, u32[]{:S(2)}) copy-start(f32[2,32,256]{2,1,0:T(8,128)} %param.22) | copy-start | bytes 196612
  346.9 7.9 copy-start.34
  347.4 7.5 copy-start.40
  347.9 6.9 copy-start.48
  354.7 54.6 %copy-start.56 = (f32[64]{0:T(128)}, f32[64]{0:T(128)S(1)}, u32[]{:S(2)}) copy-start(f32[64]{0:T(128)S(1)} %fusion.19) | copy-start | bytes 772
  411.0 2.5 copy-start.62
  412.3 179.2 %copy-start.9 = (f32[128,256]{1,0:T(8,128)}, f32[128,256]{1,0:T(8,128)S(1)}, u32[]{:S(2)}) copy-start(f32[128,256]{1,0:T(8,128)S(1)} %fusion.171) | copy-start | bytes 393220
  413.0 179.9 %copy-start.15 = (f32[128,256]{1,0:T(8,128)}, f32[128,256]{1,0:T(8,128)S(1)}, u32[]{:S(2)}) copy-start(f32[128,256]{1,0:T(8,128)S(1)} %fusion.170) | copy-start | bytes 393220
  413.4 161.8 %copy-start.26 = (f32[64,256]{1,0:T(8,128)}, f32[64,256]{1,0:T(8,128)S(1)}, u32[]{:S(2)}) copy-start(f32[64,256]{1,0:T(8,128)S(1)} %convolution_subtract_fusion.29) | copy-start | bytes 196612
  593.2 1.0 copy-start.3
  683.2 49.1 %copy-start.59 = (f32[512]{0:T(512)S(1)}, f32[512]{0:T(512)}, u32[]{:S(2)}) copy-start(f32[512]{0:T(512)} %get-tuple-element.264) | copy-start | bytes 6148
  684.4 50.7 %copy-start.46 = (f32[64,4]{0,1:T(4,128)S(1)}, f32[64,4]{0,1:T(4,128)}, u32[]{:S(2)}) copy-start(f32[64,4]{0,1:T(4,128)} %get-tuple-element.199) | copy-start | bytes 3076
  684.4 51.0 %copy-start.27 = (f32[64,256]{1,0:T(8,128)S(1)}, f32[64,256]{1,0:T(8,128)}, u32[]{:S(2)}) copy-start(f32[64,256]{1,0:T(8,128)} %copy-done.26) | copy-start | bytes 196612
  684.4 51.6 %copy-start.57 = (f32[64]{0:T(128)S(1)}, f32[64]{0:T(128)}, u32[]{:S(2)}) copy-start(f32[64]{0:T(128)} %copy-done.56) | copy-start | bytes 772
  734.2 57.2 %copy-start.36 = (f32[128,1]{0,1:T(1,128)}, f32[128,1]{0,1:T(1,128)S(1)}, u32[]{:S(2)}) copy-start(f32[128,1]{0,1:T(1,128)S(1)} %convolution_bitcast_fusion.18) | copy-start | bytes 1540
  734.6 56.7 %copy-start.42 = (f32[128,1]{0,1:T(1,128)}, f32[128,1]{0,1:T(1,128)S(1)}, u32[]{:S(2)}) copy-start(f32[128,1]{0,1:T(1,128)S(1)} %convolution_bitcast_fusion.16) | copy-start | bytes 1540
  735.2 57.3 %copy-start.50 = (f32[128,1]{0,1:T(1,128)}, f32[128,1]{0,1:T(1,128)S(1)}, u32[]{:S(2)}) copy-start(f32[128,1]{0,1:T(1,128)S(1)} %convolution_bitcast_fusion.15) | copy-start | bytes 1540
  736.3 59.9 %copy-start.54 = (f32[64]{0:T(128)}, f32[64]{0:T(128)S(1)}, u32[]{:S(2)}) copy-start(f32[64]{0:T(128)S(1)} %fusion.20) | copy-start | bytes 772
  749.5 0.7 copy-start.24
  796.1 4.7 copy-start.28
  798.8 2.5 copy-start.61
  798.8 2.5 copy-start.63
  799.6 112.0 %copy-start.5 = (f32[128,256]{1,0:T(8,128)}, f32[128,256]{1,0:T(8,128)S(1)}, u32[]{:S(2)}) copy-start(f32[128,256]{1,0:T(8,128)S(1)} %fusion.176) | copy-start | bytes 393220
  800.2 182.1 %copy-start.11 = (f32[128,256]{1,0:T(8,128)}, f32[128,256]{1,0:T(8,128)S(1)}, u32[]{:S(2)}) copy-start(f32[128,256]{1,0:T(8,128)S(1)} %fusion.175) | copy-start | bytes 393220
  800.9 110.8 %copy-start.17 = (f32[128,256]{1,0:T(8,128)}, f32[128,256]{1,0:T(8,128)S(1)}, u32[]{:S(2)}) copy-start(f32[128,256]{1,0:T(8,128)S(1)} %fusion.174) | copy-start | bytes 393220
  801.2 181.0 %copy-start.29 = (f32[64,256]{1,0:T(8,128)}, f32[64,256]{1,0:T(8,128)S(1)}, u32[]{:S(2)}) copy-start(f32[64,256]{1,0:T(8,128)S(1)} %convolution_subtract_fusion.28) | copy-start | bytes 196612
  986.1 1.0 copy-start.4
  1078.7 53.4 %copy-start.60 = (f32[512]{0:T(512)S(1)}, f32[512]{0:T(512)}, u32[]{:S(2)}) copy-start(f32[512]{0:T(512)} %get-tuple-element.262) | copy-start | bytes 6148
  1080.3 60.1 %copy-start.21 = (f32[64,512]{1,0:T(8,128)S(1)}, f32[64,512]{1,0:T(8,128)}, u32[]{:S(2)}) copy-start(f32[64,512]{1,0:T(8,128)} %fusion.3) | copy-start | bytes 393220
  1080.3 60.1 %copy-start.55 = (f32[64]{0:T(128)S(1)}, f32[64]{0:T(128)}, u32[]{:S(2)}) copy-start(f32[64]{0:T(128)} %copy-done.54) | copy-start | bytes 772
  1137.5 3.8 copy-start.38
  1138.9 2.4 copy-start.44
  1140.4 0.9 copy-start.52
  1196.4 6.7 copy-start.22
  1196.4 6.7 copy-start.30
  1198.2 7.5 copy-start.33
  1199.9 3.2 copy-start.7
  1201.4 2.8 copy-start.13
  1201.4 6.0 copy-start
  1203.1 4.2 copy-start.19
  1207.4 2.3 copy-start.35
  1207.4 2.3 copy-start.41
  1207.4 2.3 copy-start.49
  1209.7 1.2 copy-start.1
  1209.7 1.2 copy-start.10
  1209.7 1.2 copy-start.16
  1215.0 2.2 copy-start.37
  1215.0 2.2 copy-start.43
  1215.0 2.2 copy-start.51
  1217.2 1.9 copy-start.6
  1217.2 1.9 copy-start.12
  1217.2 1.9 copy-start.18
  1219.2 1.8 copy-start.47
  1221.4 2.0 copy-start.39
  1221.4 2.0 copy-start.45
  1221.4 2.0 copy-start.53
  1223.5 1.9 copy-start.58
  1223.5 2.5 copy-start.8
  1223.5 2.5 copy-start.14
  1223.5 2.5 copy-start.20
  (1 other events, 0.7 us)
where the time goes:
time: 1240 us; the launch traced here: 1230 us
  blocking collectives  547 us (44%)
  other arithmetic  488 us (39%)
  local copies, waits for them, and re-layouts  86.3 us (7%)
  matrix products  86 us (7%)
  between operations  21.1 us (2%)
    psum x3, blocking collectives, from_root(): return lax.psum(block, axis)  337 us
    another operation x44, other arithmetic, factorize(): lower_factor = jnp.linalg.cholesky(system)  239 us
    unnamed x3, blocking collectives  133 us
    another operation x7, other arithmetic, factorize(): lax.linalg.triangular_solve(lower_factor, solved, left_side=True, lower=T...  122 us
    another operation x3, other arithmetic, factorize(): lax.linalg.triangular_solve(shifted, anomalies, left_side=True, lower=True)  119 us
    all_gather x3, blocking collectives, per_device(): lax.all_gather(sent_rows, 'shard', axis=0, tiled=True)  77 us
    another operation x60, local copies, waits for them, and re-layouts, factorize(): lax.linalg.triangular_solve(shifted, anomalies, left_side=True, lower=True)  35.6 us
    another operation x67, local copies, waits for them, and re-layouts, factorize(): lax.linalg.triangular_solve(lower_factor, solved, left_side=True, lower=T...  29 us

commit v1 on v0

--- a/solution.py
+++ b/solution.py
@@ -13,7 +13,7 @@
 
 def from_root(block, axis, source):
     block = jnp.where(lax.axis_index(axis) == source, block, jnp.zeros_like(block))
-    return lax.psum(block, axis)
+    return jnp.sum(lax.all_gather(block, axis), axis=0)
 
 
 def factorize(anomalies, departs, variances):

time: 1240 us -> 1140 us (0.919)
  blocking collectives: 547 us -> 444 us
  between operations: 21.1 us -> 34.4 us
    psum x3 -> x0, blocking collectives: 337 us -> none  [from_root(): return lax.psum(block, axis)]
    unnamed x3 -> x6, blocking collectives: 133 us -> 303 us
    all_gather x0 -> x3, blocking collectives: none -> 76.5 us  [from_root(): return jnp.sum(lax.all_gather(block, axis), axis=0)]
    all_gather x3, blocking collectives: 77 us -> 64.4 us  [per_device(): lax.all_gather(sent_rows, 'shard', axis=0, tiled=True)]
  transfers between devices with their start and end apart: 0 -> 3, of which waited for: 0 -> 0; matrix products, arithmetic and copies ran while one was open for 0% -> 3% of each run, Pallas kernels for 0% -> 0%
where the time goes in v1:
time: 1140 us
  other arithmetic  491 us (43%)
  blocking collectives  444 us (39%)
  local copies, waits for them, and re-layouts  86.3 us (8%)
  matrix products  78.4 us (7%)
  between operations  34.4 us (3%)
    unnamed x6, blocking collectives  303 us
    another operation x44, other arithmetic, factorize(): lower_factor = jnp.linalg.cholesky(system)  238 us
    another operation x7, other arithmetic, factorize(): lax.linalg.triangular_solve(lower_factor, solved, left_side=True, lower=T...  123 us
    another operation x3, other arithmetic, factorize(): lax.linalg.triangular_solve(shifted, anomalies, left_side=True, lower=True)  118 us
    all_gather x3, blocking collectives, from_root(): return jnp.sum(lax.all_gather(block, axis), axis=0)  76.5 us
    all_gather x3, blocking collectives, per_device(): lax.all_gather(sent_rows, 'shard', axis=0, tiled=True)  64.4 us
    another operation x60, local copies, waits for them, and re-layouts, factorize(): lax.linalg.triangular_solve(shifted, anomalies, left_side=True, lower=True)  35.2 us
    another operation x67, local copies, waits for them, and re-layouts, factorize(): lax.linalg.triangular_solve(lower_factor, solved, left_side=True, lower=T...  25.5 us
  transfers between devices with their start and end apart: 3, of which 0 were waited for; matrix products, arithmetic and copies ran while one was open for 3% of the time, Pallas kernels for 0%

profile of v1, /device:TPU:1, one launch (start us, length us, event | category | flops | bytes accessed | tf_op | source)
XLA Modules:
  0.0 1135.6 jit_solution(17504180350228777656)
XLA Ops:
  25.0 62.1 %all-reduce.4 = f32[1024]{0:T(1024)S(1)} all-reduce(f32[1024]{0:T(1024)S(1)} %fusion.233), channel_id=5, replica_groups=mesh['region'=32,'shard'=16] {'region'}, use_global_device_ids=true, to_apply=%add.4 | all-reduce | flops 1024 | bytes 8192
  88.0 25.3 %all-gather.6 = f32[32,1,32]{2,1,0:T(1,128)S(1)} all-gather(f32[1,1,32]{2,1,0:T(1,128)S(1)} %get-tuple-element.351), channel_id=1, replica_groups=mesh['region'=32,'shard'=16] {'region'}, dimensions={0}, use_global_device_ids=true | all-gather | bytes 4224 | tf_op jit(solution)/shard_map/all_gather | solution.py:16
  113.9 51.5 %all-reduce.12 = (f32[512]{0:T(512)S(1)}, f32[512]{0:T(512)S(1)}) all-reduce(f32[512]{0:T(512)S(1)} %dynamic-update-slice.30, f32[512]{0:T(512)S(1)} %dynamic-update-slice.34), channel_id=1, replica_groups=mesh['region'=32,'shard'=16] {'shard'}, use_global_device_ids=true, to_apply=%add.1 | all-reduce | flops 1024 | bytes 8192
  173.1 25.4 %all-gather.7 = f32[32,1,32]{2,1,0:T(1,128)S(1)} all-gather(f32[1,1,32]{2,1,0:T(1,128)S(1)} %get-tuple-element.352), channel_id=1, replica_groups=mesh['region'=32,'shard'=16] {'region'}, dimensions={0}, use_global_device_ids=true | all-gather | bytes 4224 | tf_op jit(solution)/shard_map/all_gather | solution.py:16
  198.9 25.8 %all-gather.8 = f32[32,1,32]{2,1,0:T(1,128)S(1)} all-gather(f32[1,1,32]{2,1,0:T(1,128)S(1)} %get-tuple-element.350), channel_id=1, replica_groups=mesh['region'=32,'shard'=16] {'region'}, dimensions={0}, use_global_device_ids=true | all-gather | bytes 4224 | tf_op jit(solution)/shard_map/all_gather | solution.py:16
  226.3 31.8 %all_gather.77 = f32[512,256]{1,0:T(8,128)S(1)} all-gather(f32[32,256]{1,0:T(8,128)S(1)} %reduce_sum.135), channel_id=1, replica_groups=mesh['region'=32,'shard'=16] {'shard'}, dimensions={0}, use_global_device_ids=true | all-gather | bytes 557056 | tf_op jit(solution)/shard_map/all_gather | solution.py:96
  260.7 11.7 %cholesky.374 = f32[128,128]{1,0:T(8,128)S(1)} custom-call(f32[128,128]{1,0:T(8,128)S(1)} %cholesky.586), custom_call_target="Cholesky" | custom-call | tf_op jit(solution)/shard_map/jit(cholesky)/cholesky | solution.py:22
  272.4 9.8 custom-call.46
  284.8 11.7 %cholesky.393 = f32[128,128]{1,0:T(8,128)S(1)} custom-call(f32[128,128]{1,0:T(8,128)S(1)} %cholesky.590), custom_call_target="Cholesky" | custom-call | tf_op jit(solution)/shard_map/jit(cholesky)/cholesky | solution.py:22
  297.0 9.8 custom-call.47
  308.8 11.7 %cholesky.414 = f32[128,128]{1,0:T(8,128)S(1)} custom-call(f32[128,128]{1,0:T(8,128)S(1)} %cholesky.595), custom_call_target="Cholesky" | custom-call | tf_op jit(solution)/shard_map/jit(cholesky)/cholesky | solution.py:22
  320.7 9.8 custom-call.48
  332.1 11.9 %cholesky.431 = f32[128,128]{1,0:T(8,128)S(1)} custom-call(f32[128,128]{1,0:T(8,128)S(1)} %convolution_subtract_fusion.32), custom_call_target="Cholesky" | custom-call | tf_op jit(solution)/shard_map/jit(cholesky)/cholesky | solution.py:22
  349.9 11.7 %while.24 = (s32[]{:T(128)}, f32[512,512]{0,1:T(8,128)}, s32[4,2]{0,1:T(2,128)S(1)}, f32[4,128,128]{2,1,0:T(8,128)S(1)}, s32[]{:T(128)}) while((s32[]{:T(128)}, f32[512,512]{0,1:T(8,128)}, s32[4,2]{0,1:T(2,128)S(1)}, f32[4,128,128]{2,1,0:T(8,128)S(1)}, s32[]{:T(128)}) %tuple.188), condition=%wide.while_cond, body=%wide.while_body.sunk | while | flops 2 | bytes 393321 | solution.py:24
  350.5 2.2 dynamic-slice.56
  353.5 2.2 dynamic-slice.56
  356.4 2.2 dynamic-slice.56
  359.4 2.1 dynamic-slice.56
  361.7 39.3 %custom-call.49 = f32[4,128,128]{1,2,0:T(8,128)S(1)} custom-call(f32[4,128,128]{2,1,0:T(8,128)S(1)} %get-tuple-element.90), custom_call_target="InvertDiagBlocksLowerTriangular" | custom-call | tf_op jit(solution)/shard_map/triangular_solve/custom-call.3 | solution.py:24
  406.2 8.5 while.25
  414.6 39.3 %custom-call.50 = f32[4,128,128]{1,2,0:T(8,128)S(1)} custom-call(f32[4,128,128]{2,1,0:T(8,128)S(1)} %get-tuple-element.91), custom_call_target="InvertDiagBlocksLowerTriangular" | custom-call | tf_op jit(solution)/shard_map/triangular_solve/custom-call.8 | solution.py:25
  463.4 58.6 %all-reduce.6 = f32[1024]{0:T(1024)S(1)} all-reduce(f32[1024]{0:T(1024)S(1)} %fusion.234), channel_id=6, replica_groups=mesh['region'=32,'shard'=16] {'region'}, use_global_device_ids=true, to_apply=%add.6 | all-reduce | flops 1024 | bytes 8192
  522.3 37.4 %all-reduce.11 = (f32[512]{0:T(512)S(1)}, f32[512]{0:T(512)}) all-reduce(f32[512]{0:T(512)} %copy-done.24, f32[512]{0:T(512)S(1)} %dynamic-update-slice.36), channel_id=1, replica_groups=mesh['region'=32,'shard'=16] {'shard'}, use_global_device_ids=true, to_apply=%add.2 | all-reduce | flops 1024 | bytes 8192
  560.6 2.3 bitcast_multiply_fusion.2
  564.1 3.6 convolution_subtract_fusion.2
  569.0 16.4 %all_gather.82 = f32[512,256]{1,0:T(8,128)S(1)} all-gather(f32[32,256]{1,0:T(8,128)S(1)} %reduce_sum.139), channel_id=1, replica_groups=mesh['region'=32,'shard'=16] {'shard'}, dimensions={0}, use_global_device_ids=true | all-gather | bytes 557056 | tf_op jit(solution)/shard_map/all_gather | solution.py:96
  590.2 11.7 %cholesky.446 = f32[128,128]{1,0:T(8,128)S(1)} custom-call(f32[128,128]{1,0:T(8,128)S(1)} %cholesky.599), custom_call_target="Cholesky" | custom-call | tf_op jit(solution)/shard_map/jit(cholesky)/cholesky | solution.py:22
  602.0 9.8 custom-call.51
  614.3 11.7 %cholesky.465 = f32[128,128]{1,0:T(8,128)S(1)} custom-call(f32[128,128]{1,0:T(8,128)S(1)} %cholesky.603), custom_call_target="Cholesky" | custom-call | tf_op jit(solution)/shard_map/jit(cholesky)/cholesky | solution.py:22
  626.8 9.8 custom-call.52
  638.6 11.7 %cholesky.486 = f32[128,128]{1,0:T(8,128)S(1)} custom-call(f32[128,128]{1,0:T(8,128)S(1)} %cholesky.608), custom_call_target="Cholesky" | custom-call | tf_op jit(solution)/shard_map/jit(cholesky)/cholesky | solution.py:22
  650.5 9.8 custom-call.53
  662.0 11.9 %cholesky.503 = f32[128,128]{1,0:T(8,128)S(1)} custom-call(f32[128,128]{1,0:T(8,128)S(1)} %convolution_subtract_fusion.31), custom_call_target="Cholesky" | custom-call | tf_op jit(solution)/shard_map/jit(cholesky)/cholesky | solution.py:22
  682.3 11.9 %while.26 = (s32[]{:T(128)}, f32[512,512]{0,1:T(8,128)}, s32[4,2]{0,1:T(2,128)S(1)}, f32[4,128,128]{2,1,0:T(8,128)S(1)}, s32[]{:T(128)}) while((s32[]{:T(128)}, f32[512,512]{0,1:T(8,128)}, s32[4,2]{0,1:T(2,128)S(1)}, f32[4,128,128]{2,1,0:T(8,128)S(1)}, s32[]{:T(128)}) %tuple.214), condition=%wide.while_cond.clone, body=%wide.while_body.clone.sunk | while | flops 2 | bytes 393321 | solution.py:24
  682.9 2.2 dynamic-slice.60
  685.9 2.2 dynamic-slice.60
  688.9 2.2 dynamic-slice.60
  691.9 2.2 dynamic-slice.60
  694.2 39.3 %custom-call.54 = f32[4,128,128]{1,2,0:T(8,128)S(1)} custom-call(f32[4,128,128]{2,1,0:T(8,128)S(1)} %get-tuple-element.92), custom_call_target="InvertDiagBlocksLowerTriangular" | custom-call | tf_op jit(solution)/shard_map/triangular_solve/custom-call.3 | solution.py:24
  738.7 8.8 while.27
  748.2 40.1 %custom-call.55 = f32[4,128,128]{1,2,0:T(8,128)S(1)} custom-call(f32[4,128,128]{2,1,0:T(8,128)} %copy-done.7), custom_call_target="InvertDiagBlocksLowerTriangular" | custom-call | tf_op jit(solution)/shard_map/triangular_solve/custom-call.8 | solution.py:25
  797.6 55.9 %all-reduce.8 = f32[1024]{0:T(1024)S(1)} all-reduce(f32[1024]{0:T(1024)S(1)} %fusion.235), channel_id=7, replica_groups=mesh['region'=32,'shard'=16] {'region'}, use_global_device_ids=true, to_apply=%add.8 | all-reduce | flops 1024 | bytes 8192
  853.8 37.2 %all-reduce.10 = (f32[512]{0:T(512)S(1)}, f32[512]{0:T(512)S(1)}) all-reduce(f32[512]{0:T(512)} %copy-done.25, f32[512]{0:T(512)S(1)} %dynamic-update-slice.38), channel_id=1, replica_groups=mesh['region'=32,'shard'=16] {'shard'}, use_global_device_ids=true, to_apply=%add.3 | all-reduce | flops 1024 | bytes 8192
  892.1 2.0 bitcast_multiply_fusion.1
  894.1 1.9 fusion.270
  896.0 2.8 convolution_subtract_fusion.1
  900.0 16.2 %all_gather.87 = f32[512,256]{1,0:T(8,128)S(1)} all-gather(f32[32,256]{1,0:T(8,128)S(1)} %reduce_sum.143), channel_id=1, replica_groups=mesh['region'=32,'shard'=16] {'shard'}, dimensions={0}, use_global_device_ids=true | all-gather | bytes 557056 | tf_op jit(solution)/shard_map/all_gather | solution.py:96
  918.9 11.7 %cholesky.518 = f32[128,128]{1,0:T(8,128)S(1)} custom-call(f32[128,128]{1,0:T(8,128)S(1)} %cholesky.612), custom_call_target="Cholesky" | custom-call | tf_op jit(solution)/shard_map/jit(cholesky)/cholesky | solution.py:22
  930.7 9.8 custom-call.56
  943.0 11.7 %cholesky.537 = f32[128,128]{1,0:T(8,128)S(1)} custom-call(f32[128,128]{1,0:T(8,128)S(1)} %cholesky.616), custom_call_target="Cholesky" | custom-call | tf_op jit(solution)/shard_map/jit(cholesky)/cholesky | solution.py:22
  955.3 9.8 custom-call.57
  967.1 11.7 %cholesky.558 = f32[128,128]{1,0:T(8,128)S(1)} custom-call(f32[128,128]{1,0:T(8,128)S(1)} %cholesky.621), custom_call_target="Cholesky" | custom-call | tf_op jit(solution)/shard_map/jit(cholesky)/cholesky | solution.py:22
  978.9 9.8 custom-call.58
  990.4 11.9 %cholesky.575 = f32[128,128]{1,0:T(8,128)S(1)} custom-call(f32[128,128]{1,0:T(8,128)S(1)} %convolution_subtract_fusion.30), custom_call_target="Cholesky" | custom-call | tf_op jit(solution)/shard_map/jit(cholesky)/cholesky | solution.py:22
  1009.7 8.5 while.29
  1018.2 39.3 %custom-call.60 = f32[4,128,128]{1,2,0:T(8,128)S(1)} custom-call(f32[4,128,128]{2,1,0:T(8,128)S(1)} %get-tuple-element.95), custom_call_target="InvertDiagBlocksLowerTriangular" | custom-call | tf_op jit(solution)/shard_map/triangular_solve/custom-call.8 | solution.py:25
  1060.5 12.0 %while.28 = (s32[]{:T(128)}, f32[512,512]{0,1:T(8,128)}, s32[4,2]{0,1:T(2,128)S(1)}, f32[4,128,128]{2,1,0:T(8,128)S(1)}, s32[]{:T(128)}) while((s32[]{:T(128)}, f32[512,512]{0,1:T(8,128)}, s32[4,2]{0,1:T(2,128)S(1)}, f32[4,128,128]{2,1,0:T(8,128)S(1)}, s32[]{:T(128)}) %tuple.217), condition=%wide.while_cond.clone.1, body=%wide.while_body.clone.1.sunk | while | flops 2 | bytes 393321 | solution.py:24
  1061.1 2.3 dynamic-slice.64
  1064.1 2.3 dynamic-slice.64
  1067.2 2.3 dynamic-slice.64
  1070.2 2.2 dynamic-slice.64
  1072.5 39.6 %custom-call.59 = f32[4,128,128]{1,2,0:T(8,128)S(1)} custom-call(f32[4,128,128]{2,1,0:T(8,128)S(1)} %get-tuple-element.94), custom_call_target="InvertDiagBlocksLowerTriangular" | custom-call | tf_op jit(solution)/shard_map/triangular_solve/custom-call.3 | solution.py:24
  1120.9 2.0 bitcast_multiply_fusion
  1124.8 2.8 convolution_subtract_fusion
  (448 shorter events, 146.4 us)
Async XLA Ops:
  7.2 217.8 %all-gather.13.cloned.1.call-start = ((), (), s32[]{:S(2)}) async-start(), calls=%async_computation | async-start | bytes 1081344 | tf_op jit(solution)/shard_map/all_gather | solution.py:16
  12.6 555.1 %all-gather.15.cloned.1.call-start = ((), (), s32[]{:S(2)}) async-start(), calls=%async_computation.1 | async-start | bytes 1081344 | tf_op jit(solution)/shard_map/all_gather | solution.py:16
  24.4 0.6 copy-start.31
  198.9 60.5 %copy-start.24 = (f32[512]{0:T(512)}, f32[512]{0:T(512)S(1)}, u32[]{:S(2)}) copy-start(f32[512]{0:T(512)S(1)} %dynamic-update-slice.31) | copy-start | bytes 6148
  224.9 34.5 %copy-start.25 = (f32[512]{0:T(512)}, f32[512]{0:T(512)S(1)}, u32[]{:S(2)}) copy-start(f32[512]{0:T(512)S(1)} %dynamic-update-slice.32) | copy-start | bytes 6148
  259.7 1.0 copy-start.3
  414.6 41.5 %copy-start.8 = (f32[2,32,256]{2,1,0:T(8,128)S(1)}, f32[2,32,256]{2,1,0:T(8,128)}, u32[]{:S(2)}) copy-start(f32[2,32,256]{2,1,0:T(8,128)} %param.22) | copy-start | bytes 196612
  457.2 0.6 copy-start.11
  457.8 102.8 %copy-start.2 = (f32[1024,256]{1,0:T(8,128)S(1)}, f32[1024,256]{1,0:T(8,128)}, u32[]{:S(2)}) copy-start(f32[1024,256]{1,0:T(8,128)} %param.20) | copy-start | bytes 3145732
  458.4 440.3 %all-gather.17.cloned.1.call-start = ((), (), s32[]{:S(2)}) async-start(), calls=%async_computation.2 | async-start | bytes 1081344 | tf_op jit(solution)/shard_map/all_gather | solution.py:16
  460.8 1.9 copy-start.18
  461.3 1.5 copy-start.22
  462.7 0.6 copy-start.26
  560.6 2.3 copy-start.19
  560.6 2.3 copy-start.23
  589.2 1.0 copy-start.4
  626.7 47.3 %copy-start.15 = (f32[64,4]{1,0:T(8,128)S(1)}, f32[64,4]{1,0:T(8,128)}, u32[]{:S(2)}) copy-start(f32[64,4]{1,0:T(8,128)} %copy.119) | copy-start | bytes 3076
  626.7 47.4 %copy-start.12 = (f32[64,256]{1,0:T(8,128)S(1)}, f32[64,256]{1,0:T(8,128)}, u32[]{:S(2)}) copy-start(f32[64,256]{1,0:T(8,128)} %copy-done.11) | copy-start | bytes 196612
  694.2 44.5 %copy-start.1 = (f32[512,512]{0,1:T(8,128)S(1)}, f32[512,512]{0,1:T(8,128)}, u32[]{:S(2)}) copy-start(f32[512,512]{0,1:T(8,128)} %get-tuple-element.584) | copy-start | bytes 3145732
  747.5 0.7 copy-start.7
  788.4 2.1 copy-start.13
  788.4 4.6 copy-start.30
  789.5 6.5 copy-start.6
  791.7 0.6 copy-start.9
  794.9 1.9 copy-start.16
  795.4 1.4 copy-start.20
  796.8 0.6 copy-start.27
  892.0 2.0 copy-start.17
  892.1 2.0 copy-start.21
  917.9 1.0 copy-start.5
  955.1 47.3 %copy-start.14 = (f32[64,4]{1,0:T(8,128)S(1)}, f32[64,4]{1,0:T(8,128)}, u32[]{:S(2)}) copy-start(f32[64,4]{1,0:T(8,128)} %copy.140) | copy-start | bytes 3076
  955.2 47.4 %copy-start.10 = (f32[64,256]{1,0:T(8,128)S(1)}, f32[64,256]{1,0:T(8,128)}, u32[]{:S(2)}) copy-start(f32[64,256]{1,0:T(8,128)} %copy-done.9) | copy-start | bytes 196612
  1115.5 3.8 copy-start.28
  1118.6 2.3 copy-start
  1124.8 3.5 copy-start.29
Sparse Core Ops, SparseCore 0:
  12.7 82.1 all-gather.12
  458.6 70.8 all-gather.14
  793.1 67.7 all-gather.16
